TPU v7x, 512 devices: a whole 4x4x16 slice. The times are simulated.
512 devices in a mesh: dp: 16 (over z), expert: 32 (over y, x, core).
Axes of the slice: x: 4, y: 4, z: 16, core: 2. Of those that a mesh axis runs over, the one named last changes fastest.
Arguments:
- tokens: bfloat16 [4096, 4096], P('expert', 'dp'), may hold values from -6 to 6
- routing: int32 [4096, 8], P('expert'), may hold values from 0 to 31, all different within a row; in each aligned block of 128 rows (0 to 127, 128 to 255, ...) at most 40 rows name the same one
- gate_probs: float32 [4096, 8], P('expert'), may hold values from 0.05 to 0.3
- paired: int32 [32], P('expert'), may hold values from 0 to 1, as said below
- w_gate: bfloat16 [32, 4096, 768], P('expert', 'dp'), may hold values from -0.09375 to 0.09375
- w_up: bfloat16 [32, 4096, 768], P('expert', 'dp'), may hold values from -0.09375 to 0.09375
- w_down: bfloat16 [32, 768, 4096], P('expert', None, 'dp'), may hold values from -0.21875 to 0.21875
- cotangent: bfloat16 [4096, 4096], P('expert', 'dp'), may hold values from -6 to 6
Outputs:
- output: bfloat16 [4096, 4096], P('expert', 'dp')
- grad_tokens: bfloat16 [4096, 4096], P('expert', 'dp')
- grad_gate: float32 [32, 4096, 768], P('expert', 'dp')
- grad_up: float32 [32, 4096, 768], P('expert', 'dp')
- grad_down: float32 [32, 768, 4096], P('expert', None, 'dp')
Inputs may be any that keep to these rules, and one draw needn't show every extreme that they name: `routing`: each token names 8 different copies; among the tokens of one source (aligned blocks of 128 tokens) no copy is named more than 40 times, a bound that some block reaches. paired[c] equals paired[(c + 16) mod 32]; paired[0] and paired[31] are 1.
All inputs are finite; a program needn't handle non-finite values.
Results may differ from a plain program's by a relative error of at most 0.029.
Values may be sent and summed in bfloat16 or wider, within the bound.
A program may use at most 64 MiB of HBM per device.

v0:
```python
import jax
import jax.numpy as jnp
from jax import lax
from jax.sharding import PartitionSpec as P


def swapped(value, axis, stride):
    mask = 2**stride
    pairs = [(source, source ^ mask) for source in range(lax.axis_size(axis))]
    return lax.ppermute(value, axis, pairs)


def product(left, right):
    return jnp.dot(left, right, preferred_element_type=jnp.float32)


def inner_rows(left, right):
    return lax.dot_general(
        left, right, (((0,), (0,)), ((), ())), preferred_element_type=jnp.float32
    )


def outer_cols(left, right):
    return lax.dot_general(
        left, right, (((1,), (1,)), ((), ())), preferred_element_type=jnp.float32
    )


def rounded(value):
    return lax.optimization_barrier(value.astype(jnp.bfloat16)).astype(jnp.float32)


def per_device(tokens, routing, gate_probs, paired, w_gate, w_up, w_down, cotangent):
    n_expert = lax.axis_size("expert")
    n_data = lax.axis_size("dp")
    token_count, top_count = routing.shape
    slab = tokens.shape[1]
    hidden = w_gate.shape[2]
    capacity = max(2, 5 * token_count * top_count // (4 * n_expert))
    all_rows = n_expert * capacity
    own_rows = all_rows // n_data
    gate_slab = w_gate[0]
    up_slab = w_up[0]
    down_slab = w_down[0]
    flat_route = routing.reshape(token_count * top_count)
    onehot = (flat_route[:, None] == jnp.arange(n_expert, dtype=jnp.int32)[None, :]).astype(
        jnp.int32
    )
    earlier = jnp.cumsum(onehot, axis=0) - onehot
    target = flat_route * capacity + jnp.sum(earlier * onehot, axis=1)
    select = jnp.arange(all_rows, dtype=jnp.int32)[:, None] == target[None, :]
    select_grid = select.reshape(all_rows, token_count, top_count)
    token_select = jnp.any(select_grid, axis=2).astype(jnp.bfloat16)
    weight_select = jnp.sum(select_grid.astype(jnp.float32) * gate_probs[None, :, :], axis=2)
    weight_high = weight_select.astype(jnp.bfloat16)
    weight_low = (weight_select - weight_high.astype(jnp.float32)).astype(jnp.bfloat16)
    send_tokens = product(token_select, tokens).astype(jnp.bfloat16)
    scaled = (gate_probs[:, :, None] * cotangent.astype(jnp.float32)[:, None, :]).astype(
        jnp.bfloat16
    )
    send_grads = product(
        select.astype(jnp.bfloat16), scaled.reshape(token_count * top_count, slab)
    ).astype(jnp.bfloat16)
    arrived = (
        lax.all_to_all(
            send_tokens.reshape(n_expert, capacity, slab),
            "expert",
            split_axis=0,
            concat_axis=0,
            tiled=True,
        ),
        lax.all_to_all(
            send_grads.reshape(n_expert, capacity, slab),
            "expert",
            split_axis=0,
            concat_axis=0,
            tiled=True,
        ),
    )
    token_slab = arrived[0].reshape(all_rows, slab)
    grad_slab = arrived[1].reshape(all_rows, slab)
    block_rows = token_slab
    summed = lax.psum_scatter(
        rounded(
            jnp.concatenate([product(block_rows, gate_slab), product(block_rows, up_slab)], axis=1)
        ).astype(jnp.bfloat16),
        "dp",
        scatter_dimension=0,
        tiled=True,
    ).astype(jnp.float32)
    gate_own = summed[:, :hidden]
    up_own = summed[:, hidden:]
    hid_own = (jax.nn.silu(gate_own) * up_own).astype(jnp.bfloat16)
    piece = lax.all_gather(hid_own, "dp", axis=0, tiled=True)
    answer_acc = product(piece, down_slab)
    grad_down = inner_rows(piece, grad_slab)
    answer_slab = answer_acc.astype(jnp.bfloat16)
    answer_back = lax.all_to_all(
        answer_slab.reshape(n_expert, capacity, slab),
        "expert",
        split_axis=0,
        concat_axis=0,
        tiled=True,
    )
    hidden_parts = (
        outer_cols(grad_slab, down_slab).astype(jnp.bfloat16).reshape(n_data, own_rows, hidden)
    )
    arrived_parts = lax.all_to_all(hidden_parts, "dp", split_axis=0, concat_axis=0, tiled=True)
    grad_hidden = jnp.sum(arrived_parts.astype(jnp.float32), axis=0)
    sigma = jax.nn.sigmoid(gate_own)
    activated = gate_own * sigma
    grad_gate_rows = (grad_hidden * up_own * sigma * (1.0 + gate_own * (1.0 - sigma))).astype(
        jnp.bfloat16
    )
    grad_up_rows = (grad_hidden * activated).astype(jnp.bfloat16)
    piece_gate = lax.all_gather(grad_gate_rows, "dp", axis=0, tiled=True)
    piece_up = lax.all_gather(grad_up_rows, "dp", axis=0, tiled=True)
    block_rows = token_slab
    gate_acc = inner_rows(block_rows, piece_gate)
    up_acc = inner_rows(block_rows, piece_up)
    back_rows = outer_cols(piece_gate, gate_slab) + outer_cols(piece_up, up_slab)
    grad_gate = gate_acc
    grad_up = up_acc
    back_slab = back_rows.astype(jnp.bfloat16)
    back_rows_home = lax.all_to_all(
        back_slab.reshape(n_expert, capacity, slab),
        "expert",
        split_axis=0,
        concat_axis=0,
        tiled=True,
    )
    answer_home = answer_back.reshape(all_rows, slab)
    output = (inner_rows(weight_high, answer_home) + inner_rows(weight_low, answer_home)).astype(
        jnp.bfloat16
    )
    grad_tokens = inner_rows(token_select, back_rows_home.reshape(all_rows, slab)).astype(
        jnp.bfloat16
    )
    other = (
        swapped(grad_gate.astype(jnp.bfloat16), "expert", n_expert.bit_length() - 2).astype(
            grad_gate.dtype
        ),
        swapped(grad_up.astype(jnp.bfloat16), "expert", n_expert.bit_length() - 2).astype(
            grad_up.dtype
        ),
        swapped(grad_down.astype(jnp.bfloat16), "expert", n_expert.bit_length() - 2).astype(
            grad_down.dtype
        ),
    )
    keep = paired.astype(jnp.float32)[0]
    grad_gate = (grad_gate + keep * other[0])[None]
    grad_up = (grad_up + keep * other[1])[None]
    grad_down = (grad_down + keep * other[2])[None]
    return (output, grad_tokens, grad_gate, grad_up, grad_down)


def solution(mesh):
    return jax.shard_map(
        per_device,
        mesh=mesh,
        in_specs=(
            P("expert", "dp"),
            P("expert", None),
            P("expert", None),
            P("expert"),
            P("expert", "dp", None),
            P("expert", "dp", None),
            P("expert", None, "dp"),
            P("expert", "dp"),
        ),
        out_specs=(
            P("expert", "dp"),
            P("expert", "dp"),
            P("expert", "dp", None),
            P("expert", "dp", None),
            P("expert", None, "dp"),
        ),
        check_vma=False,
    )
```

profile of v0, /device:TPU:1, one launch (start us, length us, event | category | flops | bytes accessed | tf_op | source)
XLA Modules:
  0.0 480.7 jit_solution(16176602574999856850)
XLA Ops:
  7.2 0.8 copy.41
  8.2 9.0 %reduce-window.6 = s32[32,8,128]{2,1,0:T(8,128)S(1)} reduce-window(s32[32,8,128]{2,1,0:T(8,128)S(1)} %fusion.24, s32[]{:T(128)} %constant.7.clone.1), window={size=1x1x128 pad=0_0x0_0x127_0}, to_apply=%region_0.0 | reduce-window | flops 4161536 | bytes 262148 | tf_op jit(solution)/shard_map/reduce-window
  17.4 0.1 copy.43
  17.6 0.1 broadcast_add_fusion
  17.9 0.7 multiply_add_fusion.1
  18.6 4.6 fusion
  23.3 2.1 convolution_convert_fusion.4
  25.3 10.4 %all-to-all-start = ((bf16[32,40,256]{2,1,0:T(8,128)(2,1)}), bf16[32,40,256]{2,1,0:T(8,128)(2,1)S(1)}, u32[]{:S(2)}, u32[]{:S(2)}) async-start(bf16[32,40,256]{2,1,0:T(8,128)(2,1)} %bitcast.2), calls=%async_computation | async-start | bytes 1310720 | tf_op jit(solution)/shard_map/all_to_all | solution.py:65
  35.8 0.1 copy.47
  36.0 1.9 fusion.4
  38.0 10.8 %all-to-all-done = bf16[32,40,256]{2,1,0:T(8,128)(2,1)S(1)} async-done(((bf16[32,40,256]{2,1,0:T(8,128)(2,1)}), bf16[32,40,256]{2,1,0:T(8,128)(2,1)S(1)}, u32[]{:S(2)}, u32[]{:S(2)}) %all-to-all-start) | async-done | bytes 655392 | tf_op jit(solution)/shard_map/all_to_all | solution.py:65
  48.8 4.2 all-to-all-start.2
  53.1 0.7 convolution_convert_fusion.1
  53.8 0.7 convolution_convert_fusion.2
  54.5 2.1 pad_maximum_fusion
  56.7 6.3 %copy.48 = bf16[1280,1536]{1,0:T(8,128)(2,1)} copy(bf16[1280,1536]{0,1:T(8,128)(2,1)} %pad_maximum_fusion) | data formatting | bytes 7864320
  63.0 3.0 all-to-all-done.2
  66.1 0.7 convolution_convert_fusion
  66.8 117.4 %all_to_all.25 = bf16[16,80,768]{2,1,0:T(8,128)(2,1)S(1)} all-to-all(bf16[16,80,768]{2,1,0:T(8,128)(2,1)S(1)} %bitcast.77), channel_id=1, replica_groups=mesh['dp'=16,'expert'=32] {'dp'}, dimensions={0} | all-to-all | bytes 3932160 | tf_op jit(solution)/shard_map/all_to_all | solution.py:108
  184.2 0.3 convert_reduce_fusion
  184.5 27.7 %reduce-scatter.4.cloned.1.call-done = bf16[80,1536]{1,0:T(8,128)(2,1)} async-done(((bf16[1280,1536]{1,0:T(8,128)(2,1)}), bf16[80,1536]{1,0:T(8,128)(2,1)}) %reduce-scatter.4.cloned.1.call-update) | async-done | bytes 245776 | tf_op jit(solution)/shard_map/reduce_scatter | solution.py:83
  212.2 1.0 convert_element_type.90
  213.2 0.9 multiply_convert_fusion
  214.1 0.7 all-gather.6.cloned.1.call-update
  214.8 0.2 all-gather.8.cloned.1.call-start
  215.1 0.3 all-gather.8.cloned.1.call-update
  216.1 6.8 %select_reduce_fusion = f32[1280,128]{1,0:T(8,128)S(1)} fusion(f32[128,8]{0,1:T(8,128)S(1)} %copy-done.12, s32[128,8]{0,1:T(8,128)S(1)} %multiply_add_fusion.1), kind=kLoop, calls=%fused_computation.1 | loop fusion | flops 3768320 | bytes 663552 | tf_op jit(solution)/shard_map/reduce_sum | solution.py:54
  222.8 56.5 %all-gather.4.cloned.1.call-done = bf16[1280,768]{1,0:T(8,128)(2,1)} async-done(((bf16[80,768]{1,0:T(8,128)(2,1)}), bf16[1280,768]{1,0:T(8,128)(2,1)}) %all-gather.4.cloned.1.call-update) | async-done | bytes 1966096 | tf_op jit(solution)/shard_map/all_gather | solution.py:94
  279.3 3.1 convolution_convert_fusion.3
  282.4 17.4 %all-to-all-start.1 = ((bf16[32,40,256]{2,1,0:T(8,128)(2,1)}), bf16[32,40,256]{2,1,0:T(8,128)(2,1)S(1)}, u32[]{:S(2)}, u32[]{:S(2)}) async-start(bf16[32,40,256]{2,1,0:T(8,128)(2,1)} %bitcast.7), calls=%async_computation.1 | async-start | bytes 1310720 | tf_op jit(solution)/shard_map/all_to_all | solution.py:98
  299.7 52.7 %all-gather.6.cloned.1.call-done = bf16[1280,768]{1,0:T(8,128)(2,1)} async-done(((bf16[80,768]{1,0:T(8,128)(2,1)}), bf16[1280,768]{1,0:T(8,128)(2,1)}) %all-gather.6.cloned.1.call-update) | async-done | bytes 1966096 | tf_op jit(solution)/shard_map/all_gather | solution.py:116
  352.4 3.0 fusion.25
  355.4 4.6 collective-permute-start
  360.1 64.6 %all-gather.8.cloned.1.call-done = bf16[1280,768]{1,0:T(8,128)(2,1)} async-done(((bf16[80,768]{1,0:T(8,128)(2,1)}), bf16[1280,768]{1,0:T(8,128)(2,1)}) %all-gather.8.cloned.1.call-update) | async-done | bytes 1966096 | tf_op jit(solution)/shard_map/all_gather | solution.py:117
  424.7 2.4 fusion.26
  427.1 4.8 collective-permute-start.1
  431.9 1.7 fusion.27
  433.6 2.3 collective-permute-start.2
  435.9 0.7 fusion.14
  436.6 1.6 fusion.3
  438.2 2.0 add_bitcast_fusion.2
  440.2 1.0 add_bitcast_fusion.1
  441.1 18.0 %all-to-all-start.4 = ((bf16[32,40,256]{2,1,0:T(8,128)(2,1)}), bf16[32,40,256]{2,1,0:T(8,128)(2,1)}, u32[]{:S(2)}, u32[]{:S(2)}) async-start(bf16[32,40,256]{2,1,0:T(8,128)(2,1)} %bitcast.13), calls=%async_computation.4 | async-start | bytes 1310720 | tf_op jit(solution)/shard_map/all_to_all | solution.py:125
  459.1 2.0 add_bitcast_fusion
  461.1 0.3 fusion.19
  461.4 0.9 fusion.5
  462.3 9.8 %all-to-all-done.4 = bf16[32,40,256]{2,1,0:T(8,128)(2,1)} async-done(((bf16[32,40,256]{2,1,0:T(8,128)(2,1)}), bf16[32,40,256]{2,1,0:T(8,128)(2,1)}, u32[]{:S(2)}, u32[]{:S(2)}) %all-to-all-start.4) | async-done | bytes 655392 | tf_op jit(solution)/shard_map/all_to_all | solution.py:125
  472.1 2.1 convolution_convert_fusion.5
  (50 shorter events, 0.9 us)
Async XLA Ops:
  7.2 58.9 %copy-start = (bf16[1,768,256]{2,1,0:T(8,128)(2,1)S(1)}, bf16[1,768,256]{2,1,0:T(8,128)(2,1)}, u32[]{:S(2)}) copy-start(bf16[1,768,256]{2,1,0:T(8,128)(2,1)} %param.14) | copy-start | bytes 1179652
  8.0 27.8 %copy-start.11 = (bf16[128,256]{1,0:T(8,128)(2,1)S(1)}, bf16[128,256]{1,0:T(8,128)(2,1)}, u32[]{:S(2)}) copy-start(bf16[128,256]{1,0:T(8,128)(2,1)} %param.15) | copy-start | bytes 196612
  8.2 27.6 %copy-start.12 = (f32[128,8]{0,1:T(8,128)S(1)}, f32[128,8]{0,1:T(8,128)}, u32[]{:S(2)}) copy-start(f32[128,8]{0,1:T(8,128)} %param.10) | copy-start | bytes 12292
  23.3 2.1 copy-start.9
  25.3 23.5 %all-to-all-start = ((bf16[32,40,256]{2,1,0:T(8,128)(2,1)}), bf16[32,40,256]{2,1,0:T(8,128)(2,1)S(1)}, u32[]{:S(2)}, u32[]{:S(2)}) async-start(bf16[32,40,256]{2,1,0:T(8,128)(2,1)} %bitcast.2), calls=%async_computation | async-start | bytes 1310720 | tf_op jit(solution)/shard_map/all_to_all | solution.py:65
  36.0 17.1 %copy-start.6 = (bf16[1,256,768]{2,1,0:T(8,128)(2,1)S(1)}, bf16[1,256,768]{2,1,0:T(8,128)(2,1)}, u32[]{:S(2)}) copy-start(bf16[1,256,768]{2,1,0:T(8,128)(2,1)} %param.13) | copy-start | bytes 1179652
  48.8 5.0 %copy-start.5 = (bf16[1,256,768]{2,1,0:T(8,128)(2,1)S(1)}, bf16[1,256,768]{2,1,0:T(8,128)(2,1)}, u32[]{:S(2)}) copy-start(bf16[1,256,768]{2,1,0:T(8,128)(2,1)} %param.12) | copy-start | bytes 1179652
  48.8 17.3 %all-to-all-start.2 = ((bf16[32,40,256]{2,1,0:T(8,128)(2,1)}), bf16[32,40,256]{2,1,0:T(8,128)(2,1)S(1)}, u32[]{:S(2)}, u32[]{:S(2)}) async-start(bf16[32,40,256]{2,1,0:T(8,128)(2,1)} %bitcast.10), calls=%async_computation.2 | async-start | bytes 1310720 | tf_op jit(solution)/shard_map/all_to_all | solution.py:72
  53.0 159.2 %reduce-scatter.4.cloned.1.call-start = ((), (), s32[]{:S(2)}) async-start(), calls=%async_computation.9 | async-start | bytes 4177920 | tf_op jit(solution)/shard_map/reduce_scatter | solution.py:83
  63.0 216.3 %all-gather.4.cloned.1.call-start = ((), (), s32[]{:S(2)}) async-start(), calls=%async_computation.6 | async-start | bytes 2088960 | tf_op jit(solution)/shard_map/all_gather | solution.py:94
  66.1 118.1 %copy-start.3 = (bf16[32,40,256]{2,1,0:T(8,128)(2,1)}, bf16[32,40,256]{2,1,0:T(8,128)(2,1)S(1)}, u32[]{:S(2)}) copy-start(bf16[32,40,256]{2,1,0:T(8,128)(2,1)S(1)} %all-to-all-done.2) | copy-start | bytes 1966084
  214.1 138.3 %all-gather.6.cloned.1.call-start = ((), (), s32[]{:S(2)}) async-start(), calls=%async_computation.7 | async-start | bytes 2088960 | tf_op jit(solution)/shard_map/all_gather | solution.py:116
  214.8 209.8 %all-gather.8.cloned.1.call-start = ((), (), s32[]{:S(2)}) async-start(), calls=%async_computation.8 | async-start | bytes 2088960 | tf_op jit(solution)/shard_map/all_gather | solution.py:117
  282.4 158.8 %all-to-all-start.1 = ((bf16[32,40,256]{2,1,0:T(8,128)(2,1)}), bf16[32,40,256]{2,1,0:T(8,128)(2,1)S(1)}, u32[]{:S(2)}, u32[]{:S(2)}) async-start(bf16[32,40,256]{2,1,0:T(8,128)(2,1)} %bitcast.7), calls=%async_computation.1 | async-start | bytes 1310720 | tf_op jit(solution)/shard_map/all_to_all | solution.py:98
  355.4 82.8 %collective-permute-start = (bf16[256,768]{1,0:T(8,128)(2,1)}, bf16[256,768]{1,0:T(8,128)(2,1)}, u32[]{:S(2)}, u32[]{:S(2)}) collective-permute-start(bf16[256,768]{1,0:T(8,128)(2,1)} %get-tuple-element.8), channel_id=1, source_target_pairs={{0,16},{1,17},{2,18},{3,19},{4,20},{5,21},{6,22},{7,23},{8,24},{9,... | collective-permute-start | bytes 1179656 | tf_op jit(solution)/shard_map/ppermute | solution.py:10
  424.7 7.2 %copy-start.4 = (bf16[32,40,256]{2,1,0:T(8,128)(2,1)S(1)}, bf16[32,40,256]{2,1,0:T(8,128)(2,1)}, u32[]{:S(2)}) copy-start(bf16[32,40,256]{2,1,0:T(8,128)(2,1)} %copy-done.3) | copy-start | bytes 1966084
  424.7 7.2 %copy-start.13 = (bf16[1280,768]{1,0:T(8,128)(2,1)S(1)}, bf16[1280,768]{1,0:T(8,128)(2,1)}, u32[]{:S(2)}) copy-start(bf16[1280,768]{1,0:T(8,128)(2,1)} %all-gather.4.cloned.1.call-done) | copy-start | bytes 5898244
  427.1 8.8 %copy-start.1 = (bf16[1280,768]{1,0:T(8,128)(2,1)S(1)}, bf16[1280,768]{1,0:T(8,128)(2,1)}, u32[]{:S(2)}) copy-start(bf16[1280,768]{1,0:T(8,128)(2,1)} %all-gather.6.cloned.1.call-done) | copy-start | bytes 5898244
  427.1 13.1 %collective-permute-start.1 = (bf16[256,768]{1,0:T(8,128)(2,1)S(1)}, bf16[256,768]{1,0:T(8,128)(2,1)S(1)}, u32[]{:S(2)}, u32[]{:S(2)}) collective-permute-start(bf16[256,768]{1,0:T(8,128)(2,1)S(1)} %get-tuple-element.10), channel_id=1, source_target_pairs={{0,16},{1,17},{2,18},{3,19},{4,20},{5,21},{6,22},{7,23},{8,24},{9,... | collective-permute-start | bytes 1179656 | tf_op jit(solution)/shard_map/ppermute | solution.py:10
  433.6 3.0 copy-start.2
  433.6 3.0 copy-start.7
  433.6 25.5 %collective-permute-start.2 = (bf16[768,256]{1,0:T(8,128)(2,1)}, bf16[768,256]{1,0:T(8,128)(2,1)}, u32[]{:S(2)}, u32[]{:S(2)}) collective-permute-start(bf16[768,256]{1,0:T(8,128)(2,1)} %get-tuple-element.12), channel_id=1, source_target_pairs={{0,16},{1,17},{2,18},{3,19},{4,20},{5,21},{6,22},{7,23},{8,24},{9,... | collective-permute-start | bytes 1179656 | tf_op jit(solution)/shard_map/ppermute | solution.py:10
  440.2 19.0 %copy-start.8 = (f32[768,256]{1,0:T(8,128)S(1)}, f32[768,256]{1,0:T(8,128)}, u32[]{:S(2)}) copy-start(f32[768,256]{1,0:T(8,128)} %get-tuple-element.13) | copy-start | bytes 2359300
  441.1 30.9 %all-to-all-start.4 = ((bf16[32,40,256]{2,1,0:T(8,128)(2,1)}), bf16[32,40,256]{2,1,0:T(8,128)(2,1)}, u32[]{:S(2)}, u32[]{:S(2)}) async-start(bf16[32,40,256]{2,1,0:T(8,128)(2,1)} %bitcast.13), calls=%async_computation.4 | async-start | bytes 1310720 | tf_op jit(solution)/shard_map/all_to_all | solution.py:125
  461.1 11.0 %copy-start.10 = (pred[1280,128]{1,0:T(8,128)(4,1)S(1)}, pred[1280,128]{1,0:T(8,128)(4,1)}, u32[]{:S(2)}) copy-start(pred[1280,128]{1,0:T(8,128)(4,1)} %copy-done.9) | copy-start | bytes 491524
Sparse Core Ops, SparseCore 0:
  63.1 149.0 reduce-scatter.3
  214.5 64.7 all-gather.3
  282.1 70.2 all-gather.5
  355.2 69.4 all-gather.7
where the time goes:
time: 482 us; the launch traced here: 481 us
  waiting for transfers between devices  226 us (47%)
  blocking collectives  117 us (24%)
  starting transfers between devices  62 us (13%)
  other arithmetic  30.5 us (6%)
  matrix products  22 us (5%)
  between operations  14.7 us (3%)
  local copies, waits for them, and re-layouts  7.99 us (2%)
    all_to_all x1, blocking collectives, per_device(): lax.all_to_all(hidden_parts, 'dp', split_axis=0, concat_axis=0, tiled=True)  117 us
    all_gather x1, waiting for transfers between devices, per_device(): piece_up = lax.all_gather(grad_up_rows, 'dp', axis=0, tiled=True)  64.6 us
    all_gather x1, waiting for transfers between devices, per_device(): piece = lax.all_gather(hid_own, 'dp', axis=0, tiled=True)  56.5 us
    all_gather x1, waiting for transfers between devices, per_device(): piece_gate = lax.all_gather(grad_gate_rows, 'dp', axis=0, tiled=True)  52.7 us
    reduce_scatter x1, waiting for transfers between devices, per_device(): lax.psum_scatter(rounded(jnp.concatenate([product(block_rows, gate_slab),...  27.7 us
    all_to_all x1, starting transfers between devices, per_device(): lax.all_to_all(back_slab.reshape(n_expert, capacity, slab), 'expert', spl...  18 us
    all_to_all x1, starting transfers between devices, per_device(): lax.all_to_all(answer_slab.reshape(n_expert, capacity, slab), 'expert', s...  17.4 us
    ppermute x3, starting transfers between devices, swapped(): return lax.ppermute(value, axis, pairs)  11.7 us
  transfers between devices with their start and end apart: 11, of which 7 were waited for; matrix products, arithmetic and copies ran while one was open for 8% of the time, Pallas kernels for 0%

commit v1 on v0

--- a/solution.py
+++ b/solution.py
@@ -114,7 +114,12 @@
     )
     grad_up_rows = (grad_hidden * activated).astype(jnp.bfloat16)
     piece_gate = lax.all_gather(grad_gate_rows, "dp", axis=0, tiled=True)
-    piece_up = lax.all_gather(grad_up_rows, "dp", axis=0, tiled=True)
+    ring = [grad_up_rows]
+    for hop in range(15):
+        ring.append(lax.ppermute(ring[-1], "dp", [(dev, (dev + 1) % 16) for dev in range(16)]))
+    piece_up = jnp.roll(
+        jnp.concatenate(ring[::-1], axis=0), (lax.axis_index("dp") + 1) * ring[0].shape[0], axis=0
+    )
     block_rows = token_slab
     gate_acc = inner_rows(block_rows, piece_gate)
     up_acc = inner_rows(block_rows, piece_up)

time: 482 us -> 451 us (0.936)
  waiting for transfers between devices: 226 us -> 154 us
  starting transfers between devices: 62 us -> 99.8 us
    ppermute x0 -> x15, waiting for transfers between devices: none -> 81.8 us  [per_device(): lax.ppermute(ring[-1], 'dp', [(dev, (dev + 1) % 16) for dev in range(16)])]
    all_gather x1 -> x0, waiting for transfers between devices: 64.6 us -> none  [per_device(): piece_up = lax.all_gather(grad_up_rows, 'dp', axis=0, tiled=True)]
    all_gather x1, waiting for transfers between devices: 52.7 us -> 0.01 us  [per_device(): piece_gate = lax.all_gather(grad_gate_rows, 'dp', axis=0, tiled=True)]
    all_gather x1, waiting for transfers between devices: 56.5 us -> 23.6 us  [per_device(): piece = lax.all_gather(hid_own, 'dp', axis=0, tiled=True)]
    ppermute x0 -> x15, starting transfers between devices: none -> 31 us  [per_device(): lax.ppermute(ring[-1], 'dp', [(dev, (dev + 1) % 16) for dev in range(16)])]
    all_to_all x1, waiting for transfers between devices: 9.76 us -> 0.01 us  [per_device(): lax.all_to_all(back_slab.reshape(n_expert, capacity, slab), 'expert', spl...]
    all_to_all x1, waiting for transfers between devices: 0.01 us -> 6.86 us  [per_device(): lax.all_to_all(answer_slab.reshape(n_expert, capacity, slab), 'expert', s...]
    all_to_all x1, starting transfers between devices: 18 us -> 24.2 us  [per_device(): lax.all_to_all(back_slab.reshape(n_expert, capacity, slab), 'expert', spl...]
  transfers between devices with their start and end apart: 11 -> 25, of which waited for: 7 -> 20; matrix products, arithmetic and copies ran while one was open for 8% -> 9% of each run, Pallas kernels for 0% -> 0%
where the time goes in v1:
time: 451 us; the launch traced here: 450 us
  waiting for transfers between devices  154 us (34%)
  blocking collectives  117 us (26%)
  starting transfers between devices  99.8 us (22%)
  other arithmetic  31.3 us (7%)
  matrix products  22.4 us (5%)
  between operations  15.1 us (3%)
  local copies, waits for them, and re-layouts  10.2 us (2%)
    all_to_all x1, blocking collectives, per_device(): lax.all_to_all(hidden_parts, 'dp', split_axis=0, concat_axis=0, tiled=True)  117 us
    ppermute x15, waiting for transfers between devices, per_device(): lax.ppermute(ring[-1], 'dp', [(dev, (dev + 1) % 16) for dev in range(16)])  81.8 us
    ppermute x15, starting transfers between devices, per_device(): lax.ppermute(ring[-1], 'dp', [(dev, (dev + 1) % 16) for dev in range(16)])  31 us
    reduce_scatter x1, waiting for transfers between devices, per_device(): lax.psum_scatter(rounded(jnp.concatenate([product(block_rows, gate_slab),...  27.7 us
    all_to_all x1, starting transfers between devices, per_device(): lax.all_to_all(back_slab.reshape(n_expert, capacity, slab), 'expert', spl...  24.2 us
    all_gather x1, waiting for transfers between devices, per_device(): piece = lax.all_gather(hid_own, 'dp', axis=0, tiled=True)  23.6 us
    ppermute x3, starting transfers between devices, swapped(): return lax.ppermute(value, axis, pairs)  15 us
    all_to_all x1, starting transfers between devices, per_device(): lax.all_to_all(answer_slab.reshape(n_expert, capacity, slab), 'expert', s...  14.9 us
  transfers between devices with their start and end apart: 25, of which 20 were waited for; matrix products, arithmetic and copies ran while one was open for 9% of the time, Pallas kernels for 0%

profile of v1, /device:TPU:1, one launch (start us, length us, event | category | flops | bytes accessed | tf_op | source)
XLA Modules:
  0.0 450.0 jit_solution(10655276451003950678)
XLA Ops:
  8.2 9.0 %reduce-window.6 = s32[32,8,128]{2,1,0:T(8,128)S(1)} reduce-window(s32[32,8,128]{2,1,0:T(8,128)S(1)} %fusion.27, s32[]{:T(128)} %constant.35.clone.1), window={size=1x1x128 pad=0_0x0_0x127_0}, to_apply=%region_0.0 | reduce-window | flops 4161536 | bytes 262148 | tf_op jit(solution)/shard_map/reduce-window
  18.6 4.6 %fusion = pred[1280,128]{1,0:T(8,128)(4,1)S(1)} fusion(s32[128,8]{0,1:T(8,128)S(1)} %multiply_add_fusion.1), kind=kLoop, calls=%fused_computation.3 | loop fusion | flops 2457600 | bytes 167936 | tf_op jit(solution)/shard_map/reduce_or | solution.py:53
  23.3 2.1 convolution_convert_fusion.4
  25.4 10.4 %all-to-all-start = ((bf16[32,40,256]{2,1,0:T(8,128)(2,1)}), bf16[32,40,256]{2,1,0:T(8,128)(2,1)S(1)}, u32[]{:S(2)}, u32[]{:S(2)}) async-start(bf16[32,40,256]{2,1,0:T(8,128)(2,1)} %bitcast.2), calls=%async_computation | async-start | bytes 1310720 | tf_op jit(solution)/shard_map/all_to_all | solution.py:65
  36.0 2.0 fusion.4
  38.0 10.8 %all-to-all-done = bf16[32,40,256]{2,1,0:T(8,128)(2,1)S(1)} async-done(((bf16[32,40,256]{2,1,0:T(8,128)(2,1)}), bf16[32,40,256]{2,1,0:T(8,128)(2,1)S(1)}, u32[]{:S(2)}, u32[]{:S(2)}) %all-to-all-start) | async-done | bytes 655392 | tf_op jit(solution)/shard_map/all_to_all | solution.py:65
  48.8 4.1 all-to-all-start.2
  54.4 2.1 pad_maximum_fusion
  56.6 6.3 %copy.48 = bf16[1280,1536]{1,0:T(8,128)(2,1)} copy(bf16[1280,1536]{0,1:T(8,128)(2,1)} %pad_maximum_fusion) | data formatting | bytes 7864320
  62.9 3.0 all-to-all-done.2
  66.7 117.4 %all_to_all.25 = bf16[16,80,768]{2,1,0:T(8,128)(2,1)S(1)} all-to-all(bf16[16,80,768]{2,1,0:T(8,128)(2,1)S(1)} %bitcast.75), channel_id=1, replica_groups=mesh['dp'=16,'expert'=32] {'dp'}, dimensions={0} | all-to-all | bytes 3932160 | tf_op jit(solution)/shard_map/all_to_all | solution.py:108
  184.3 27.7 %reduce-scatter.4.cloned.1.call-done = bf16[80,1536]{1,0:T(8,128)(2,1)} async-done(((bf16[1280,1536]{1,0:T(8,128)(2,1)}), bf16[80,1536]{1,0:T(8,128)(2,1)}) %reduce-scatter.4.cloned.1.call-update) | async-done | bytes 245776 | tf_op jit(solution)/shard_map/reduce_scatter | solution.py:83
  213.9 3.6 collective-permute-start
  217.5 3.2 collective-permute-done
  220.7 2.4 collective-permute-start.1
  223.1 4.7 %collective-permute-done.1 = bf16[80,768]{1,0:T(8,128)(2,1)S(1)} collective-permute-done((bf16[80,768]{1,0:T(8,128)(2,1)S(1)}, bf16[80,768]{1,0:T(8,128)(2,1)S(1)}, u32[]{:S(2)}, u32[]{:S(2)}) %collective-permute-start.1) | collective-permute-done | bytes 122912 | tf_op jit(solution)/shard_map/ppermute | solution.py:119
  227.8 1.9 collective-permute-start.2
  229.8 6.4 %collective-permute-done.2 = bf16[80,768]{1,0:T(8,128)(2,1)S(1)} collective-permute-done((bf16[80,768]{1,0:T(8,128)(2,1)S(1)}, bf16[80,768]{1,0:T(8,128)(2,1)S(1)}, u32[]{:S(2)}, u32[]{:S(2)}) %collective-permute-start.2) | collective-permute-done | bytes 122912 | tf_op jit(solution)/shard_map/ppermute | solution.py:119
  238.1 7.9 %collective-permute-done.3 = bf16[80,768]{1,0:T(8,128)(2,1)S(1)} collective-permute-done((bf16[80,768]{1,0:T(8,128)(2,1)S(1)}, bf16[80,768]{1,0:T(8,128)(2,1)S(1)}, u32[]{:S(2)}, u32[]{:S(2)}) %collective-permute-start.3) | collective-permute-done | bytes 122912 | tf_op jit(solution)/shard_map/ppermute | solution.py:119
  247.9 5.6 %collective-permute-done.4 = bf16[80,768]{1,0:T(8,128)(2,1)S(1)} collective-permute-done((bf16[80,768]{1,0:T(8,128)(2,1)S(1)}, bf16[80,768]{1,0:T(8,128)(2,1)S(1)}, u32[]{:S(2)}, u32[]{:S(2)}) %collective-permute-start.4) | collective-permute-done | bytes 122912 | tf_op jit(solution)/shard_map/ppermute | solution.py:119
  253.5 2.0 collective-permute-start.5
  255.5 5.1 %collective-permute-done.5 = bf16[80,768]{1,0:T(8,128)(2,1)S(1)} collective-permute-done((bf16[80,768]{1,0:T(8,128)(2,1)S(1)}, bf16[80,768]{1,0:T(8,128)(2,1)S(1)}, u32[]{:S(2)}, u32[]{:S(2)}) %collective-permute-start.5) | collective-permute-done | bytes 122912 | tf_op jit(solution)/shard_map/ppermute | solution.py:119
  260.7 1.9 collective-permute-start.6
  262.6 5.9 %collective-permute-done.6 = bf16[80,768]{1,0:T(8,128)(2,1)S(1)} collective-permute-done((bf16[80,768]{1,0:T(8,128)(2,1)S(1)}, bf16[80,768]{1,0:T(8,128)(2,1)S(1)}, u32[]{:S(2)}, u32[]{:S(2)}) %collective-permute-start.6) | collective-permute-done | bytes 122912 | tf_op jit(solution)/shard_map/ppermute | solution.py:119
  270.4 5.7 %collective-permute-done.7 = bf16[80,768]{1,0:T(8,128)(2,1)S(1)} collective-permute-done((bf16[80,768]{1,0:T(8,128)(2,1)S(1)}, bf16[80,768]{1,0:T(8,128)(2,1)S(1)}, u32[]{:S(2)}, u32[]{:S(2)}) %collective-permute-start.7) | collective-permute-done | bytes 122912 | tf_op jit(solution)/shard_map/ppermute | solution.py:119
  276.0 1.9 collective-permute-start.8
  277.9 5.7 %collective-permute-done.8 = bf16[80,768]{1,0:T(8,128)(2,1)S(1)} collective-permute-done((bf16[80,768]{1,0:T(8,128)(2,1)S(1)}, bf16[80,768]{1,0:T(8,128)(2,1)S(1)}, u32[]{:S(2)}, u32[]{:S(2)}) %collective-permute-start.8) | collective-permute-done | bytes 122912 | tf_op jit(solution)/shard_map/ppermute | solution.py:119
  283.6 1.9 collective-permute-start.9
  285.6 6.2 %collective-permute-done.9 = bf16[80,768]{1,0:T(8,128)(2,1)S(1)} collective-permute-done((bf16[80,768]{1,0:T(8,128)(2,1)S(1)}, bf16[80,768]{1,0:T(8,128)(2,1)S(1)}, u32[]{:S(2)}, u32[]{:S(2)}) %collective-permute-start.9) | collective-permute-done | bytes 122912 | tf_op jit(solution)/shard_map/ppermute | solution.py:119
  293.7 5.9 %collective-permute-done.10 = bf16[80,768]{1,0:T(8,128)(2,1)S(1)} collective-permute-done((bf16[80,768]{1,0:T(8,128)(2,1)S(1)}, bf16[80,768]{1,0:T(8,128)(2,1)S(1)}, u32[]{:S(2)}, u32[]{:S(2)}) %collective-permute-start.10) | collective-permute-done | bytes 122912 | tf_op jit(solution)/shard_map/ppermute | solution.py:119
  301.4 4.9 %collective-permute-done.11 = bf16[80,768]{1,0:T(8,128)(2,1)S(1)} collective-permute-done((bf16[80,768]{1,0:T(8,128)(2,1)S(1)}, bf16[80,768]{1,0:T(8,128)(2,1)S(1)}, u32[]{:S(2)}, u32[]{:S(2)}) %collective-permute-start.11) | collective-permute-done | bytes 122912 | tf_op jit(solution)/shard_map/ppermute | solution.py:119
  308.3 4.9 %collective-permute-done.12 = bf16[80,768]{1,0:T(8,128)(2,1)S(1)} collective-permute-done((bf16[80,768]{1,0:T(8,128)(2,1)S(1)}, bf16[80,768]{1,0:T(8,128)(2,1)S(1)}, u32[]{:S(2)}, u32[]{:S(2)}) %collective-permute-start.12) | collective-permute-done | bytes 122912 | tf_op jit(solution)/shard_map/ppermute | solution.py:119
  315.1 4.9 %collective-permute-done.13 = bf16[80,768]{1,0:T(8,128)(2,1)S(1)} collective-permute-done((bf16[80,768]{1,0:T(8,128)(2,1)S(1)}, bf16[80,768]{1,0:T(8,128)(2,1)S(1)}, u32[]{:S(2)}, u32[]{:S(2)}) %collective-permute-start.13) | collective-permute-done | bytes 122912 | tf_op jit(solution)/shard_map/ppermute | solution.py:119
  322.0 4.9 %collective-permute-done.14 = bf16[80,768]{1,0:T(8,128)(2,1)S(1)} collective-permute-done((bf16[80,768]{1,0:T(8,128)(2,1)S(1)}, bf16[80,768]{1,0:T(8,128)(2,1)S(1)}, u32[]{:S(2)}, u32[]{:S(2)}) %collective-permute-start.14) | collective-permute-done | bytes 122912 | tf_op jit(solution)/shard_map/ppermute | solution.py:119
  330.1 5.4 %collective-permute-start.16 = (bf16[256,768]{1,0:T(8,128)(2,1)S(1)}, bf16[256,768]{1,0:T(8,128)(2,1)S(1)}, u32[]{:S(2)}, u32[]{:S(2)}) collective-permute-start(bf16[256,768]{1,0:T(8,128)(2,1)S(1)} %get-tuple-element.10), channel_id=1, source_target_pairs={{0,16},{1,17},{2,18},{3,19},{4,20},{5,21},{6,22},{7,23},{8,24},{9,... | collective-permute-start | bytes 1179656 | tf_op jit(solution)/shard_map/ppermute | solution.py:10
  336.1 7.6 %select_reduce_fusion = f32[1280,128]{1,0:T(8,128)} fusion(f32[128,8]{0,1:T(8,128)S(1)} %copy-done.12, s32[128,8]{0,1:T(8,128)S(1)} %multiply_add_fusion.1), kind=kLoop, calls=%fused_computation.1 | loop fusion | flops 3768320 | bytes 663552 | tf_op jit(solution)/shard_map/reduce_sum | solution.py:54
  344.7 2.4 fusion.17
  347.1 3.2 fusion.3
  350.3 24.2 %all-to-all-start.4 = ((bf16[32,40,256]{2,1,0:T(8,128)(2,1)}), bf16[32,40,256]{2,1,0:T(8,128)(2,1)}, u32[]{:S(2)}, u32[]{:S(2)}) async-start(bf16[32,40,256]{2,1,0:T(8,128)(2,1)} %bitcast.78), calls=%async_computation.4 | async-start | bytes 1310720 | tf_op jit(solution)/shard_map/all_to_all | solution.py:130
  376.3 4.9 %collective-permute-start.15 = (bf16[256,768]{1,0:T(8,128)(2,1)}, bf16[256,768]{1,0:T(8,128)(2,1)}, u32[]{:S(2)}, u32[]{:S(2)}) collective-permute-start(bf16[256,768]{1,0:T(8,128)(2,1)} %get-tuple-element.8), channel_id=1, source_target_pairs={{0,16},{1,17},{2,18},{3,19},{4,20},{5,21},{6,22},{7,23},{8,24},{9,... | collective-permute-start | bytes 1179656 | tf_op jit(solution)/shard_map/ppermute | solution.py:10
  381.2 23.6 %all-gather.3.cloned.1.call-done = bf16[1280,768]{1,0:T(8,128)(2,1)} async-done(((bf16[80,768]{1,0:T(8,128)(2,1)}), bf16[1280,768]{1,0:T(8,128)(2,1)}) %all-gather.3.cloned.1.call-update) | async-done | bytes 1966096 | tf_op jit(solution)/shard_map/all_gather | solution.py:94
  404.8 3.3 fusion.32
  408.1 4.7 %collective-permute-start.17 = (bf16[768,256]{1,0:T(8,128)(2,1)}, bf16[768,256]{1,0:T(8,128)(2,1)}, u32[]{:S(2)}, u32[]{:S(2)}) collective-permute-start(bf16[768,256]{1,0:T(8,128)(2,1)} %get-tuple-element.12), channel_id=1, source_target_pairs={{0,16},{1,17},{2,18},{3,19},{4,20},{5,21},{6,22},{7,23},{8,24},{9,... | collective-permute-start | bytes 1179656 | tf_op jit(solution)/shard_map/ppermute | solution.py:10
  414.4 14.9 %all-to-all-start.1 = ((bf16[32,40,256]{2,1,0:T(8,128)(2,1)}), bf16[32,40,256]{2,1,0:T(8,128)(2,1)S(1)}, u32[]{:S(2)}, u32[]{:S(2)}) async-start(bf16[32,40,256]{2,1,0:T(8,128)(2,1)} %bitcast.81), calls=%async_computation.1 | async-start | bytes 1310720 | tf_op jit(solution)/shard_map/all_to_all | solution.py:98
  429.3 2.0 add_bitcast_fusion.2
  431.3 2.0 add_bitcast_fusion
  433.2 2.1 convolution_convert_fusion.5
  435.3 6.9 %all-to-all-done.1 = bf16[32,40,256]{2,1,0:T(8,128)(2,1)S(1)} async-done(((bf16[32,40,256]{2,1,0:T(8,128)(2,1)}), bf16[32,40,256]{2,1,0:T(8,128)(2,1)S(1)}, u32[]{:S(2)}, u32[]{:S(2)}) %all-to-all-start.1) | async-done | bytes 655392 | tf_op jit(solution)/shard_map/all_to_all | solution.py:98
  (109 shorter events, 30.7 us)
Async XLA Ops:
  7.2 46.5 %copy-start = (bf16[1,256,768]{2,1,0:T(8,128)(2,1)S(1)}, bf16[1,256,768]{2,1,0:T(8,128)(2,1)}, u32[]{:S(2)}) copy-start(bf16[1,256,768]{2,1,0:T(8,128)(2,1)} %param.12) | copy-start | bytes 1179652
  7.2 28.6 %copy-start.11 = (bf16[128,256]{1,0:T(8,128)(2,1)S(1)}, bf16[128,256]{1,0:T(8,128)(2,1)}, u32[]{:S(2)}) copy-start(bf16[128,256]{1,0:T(8,128)(2,1)} %param.15) | copy-start | bytes 196612
  7.2 28.6 %copy-start.12 = (f32[128,8]{0,1:T(8,128)S(1)}, f32[128,8]{0,1:T(8,128)}, u32[]{:S(2)}) copy-start(f32[128,8]{0,1:T(8,128)} %param.10) | copy-start | bytes 12292
  23.3 2.1 copy-start.7
  23.3 29.7 %copy-start.6 = (bf16[1,256,768]{2,1,0:T(8,128)(2,1)S(1)}, bf16[1,256,768]{2,1,0:T(8,128)(2,1)}, u32[]{:S(2)}) copy-start(bf16[1,256,768]{2,1,0:T(8,128)(2,1)} %param.13) | copy-start | bytes 1179652
  25.4 23.5 %all-to-all-start = ((bf16[32,40,256]{2,1,0:T(8,128)(2,1)}), bf16[32,40,256]{2,1,0:T(8,128)(2,1)S(1)}, u32[]{:S(2)}, u32[]{:S(2)}) async-start(bf16[32,40,256]{2,1,0:T(8,128)(2,1)} %bitcast.2), calls=%async_computation | async-start | bytes 1310720 | tf_op jit(solution)/shard_map/all_to_all | solution.py:65
  48.8 17.1 %all-to-all-start.2 = ((bf16[32,40,256]{2,1,0:T(8,128)(2,1)}), bf16[32,40,256]{2,1,0:T(8,128)(2,1)S(1)}, u32[]{:S(2)}, u32[]{:S(2)}) async-start(bf16[32,40,256]{2,1,0:T(8,128)(2,1)} %bitcast.10), calls=%async_computation.2 | async-start | bytes 1310720 | tf_op jit(solution)/shard_map/all_to_all | solution.py:72
  52.9 159.1 %reduce-scatter.4.cloned.1.call-start = ((), (), s32[]{:S(2)}) async-start(), calls=%async_computation.8 | async-start | bytes 4177920 | tf_op jit(solution)/shard_map/reduce_scatter | solution.py:83
  62.9 3.1 copy-start.9
  62.9 281.8 %all-gather.5.cloned.1.call-start = ((), (), s32[]{:S(2)}) async-start(), calls=%async_computation.7 | async-start | bytes 2088960 | tf_op jit(solution)/shard_map/all_gather | solution.py:116
  65.9 118.4 %copy-start.5 = (bf16[32,40,256]{2,1,0:T(8,128)(2,1)}, bf16[32,40,256]{2,1,0:T(8,128)(2,1)S(1)}, u32[]{:S(2)}) copy-start(bf16[32,40,256]{2,1,0:T(8,128)(2,1)S(1)} %all-to-all-done.2) | copy-start | bytes 1966084
  213.8 191.0 %all-gather.3.cloned.1.call-start = ((), (), s32[]{:S(2)}) async-start(), calls=%async_computation.6 | async-start | bytes 2088960 | tf_op jit(solution)/shard_map/all_gather | solution.py:94
  213.9 6.8 %collective-permute-start = (bf16[80,768]{1,0:T(8,128)(2,1)S(1)}, bf16[80,768]{1,0:T(8,128)(2,1)S(1)}, u32[]{:S(2)}, u32[]{:S(2)}) collective-permute-start(bf16[80,768]{1,0:T(8,128)(2,1)S(1)} %get-tuple-element.5), channel_id=1, source_target_pairs={{0,32},{32,64},{64,96},{96,128},{128,160},{160,192},{192,224},{224... | collective-permute-start | bytes 368648 | tf_op jit(solution)/shard_map/ppermute | solution.py:119
  220.7 7.1 %collective-permute-start.1 = (bf16[80,768]{1,0:T(8,128)(2,1)S(1)}, bf16[80,768]{1,0:T(8,128)(2,1)S(1)}, u32[]{:S(2)}, u32[]{:S(2)}) collective-permute-start(bf16[80,768]{1,0:T(8,128)(2,1)S(1)} %collective-permute-done), channel_id=1, source_target_pairs={{0,32},{32,64},{64,96},{96,128},{128,160},{160,192},{192,224},{224... | collective-permute-start | bytes 368648 | tf_op jit(solution)/shard_map/ppermute | solution.py:119
  227.8 8.3 %collective-permute-start.2 = (bf16[80,768]{1,0:T(8,128)(2,1)S(1)}, bf16[80,768]{1,0:T(8,128)(2,1)S(1)}, u32[]{:S(2)}, u32[]{:S(2)}) collective-permute-start(bf16[80,768]{1,0:T(8,128)(2,1)S(1)} %collective-permute-done.1), channel_id=1, source_target_pairs={{0,32},{32,64},{64,96},{96,128},{128,160},{160,192},{192,224},{224... | collective-permute-start | bytes 368648 | tf_op jit(solution)/shard_map/ppermute | solution.py:119
  236.1 9.8 %collective-permute-start.3 = (bf16[80,768]{1,0:T(8,128)(2,1)S(1)}, bf16[80,768]{1,0:T(8,128)(2,1)S(1)}, u32[]{:S(2)}, u32[]{:S(2)}) collective-permute-start(bf16[80,768]{1,0:T(8,128)(2,1)S(1)} %collective-permute-done.2), channel_id=1, source_target_pairs={{0,32},{32,64},{64,96},{96,128},{128,160},{160,192},{192,224},{224... | collective-permute-start | bytes 368648 | tf_op jit(solution)/shard_map/ppermute | solution.py:119
  246.0 7.6 %collective-permute-start.4 = (bf16[80,768]{1,0:T(8,128)(2,1)S(1)}, bf16[80,768]{1,0:T(8,128)(2,1)S(1)}, u32[]{:S(2)}, u32[]{:S(2)}) collective-permute-start(bf16[80,768]{1,0:T(8,128)(2,1)S(1)} %collective-permute-done.3), channel_id=1, source_target_pairs={{0,32},{32,64},{64,96},{96,128},{128,160},{160,192},{192,224},{224... | collective-permute-start | bytes 368648 | tf_op jit(solution)/shard_map/ppermute | solution.py:119
  253.5 7.2 %collective-permute-start.5 = (bf16[80,768]{1,0:T(8,128)(2,1)S(1)}, bf16[80,768]{1,0:T(8,128)(2,1)S(1)}, u32[]{:S(2)}, u32[]{:S(2)}) collective-permute-start(bf16[80,768]{1,0:T(8,128)(2,1)S(1)} %collective-permute-done.4), channel_id=1, source_target_pairs={{0,32},{32,64},{64,96},{96,128},{128,160},{160,192},{192,224},{224... | collective-permute-start | bytes 368648 | tf_op jit(solution)/shard_map/ppermute | solution.py:119
  260.7 7.8 %collective-permute-start.6 = (bf16[80,768]{1,0:T(8,128)(2,1)S(1)}, bf16[80,768]{1,0:T(8,128)(2,1)S(1)}, u32[]{:S(2)}, u32[]{:S(2)}) collective-permute-start(bf16[80,768]{1,0:T(8,128)(2,1)S(1)} %collective-permute-done.5), channel_id=1, source_target_pairs={{0,32},{32,64},{64,96},{96,128},{128,160},{160,192},{192,224},{224... | collective-permute-start | bytes 368648 | tf_op jit(solution)/shard_map/ppermute | solution.py:119
  268.4 7.6 %collective-permute-start.7 = (bf16[80,768]{1,0:T(8,128)(2,1)S(1)}, bf16[80,768]{1,0:T(8,128)(2,1)S(1)}, u32[]{:S(2)}, u32[]{:S(2)}) collective-permute-start(bf16[80,768]{1,0:T(8,128)(2,1)S(1)} %collective-permute-done.6), channel_id=1, source_target_pairs={{0,32},{32,64},{64,96},{96,128},{128,160},{160,192},{192,224},{224... | collective-permute-start | bytes 368648 | tf_op jit(solution)/shard_map/ppermute | solution.py:119
  276.0 7.6 %collective-permute-start.8 = (bf16[80,768]{1,0:T(8,128)(2,1)S(1)}, bf16[80,768]{1,0:T(8,128)(2,1)S(1)}, u32[]{:S(2)}, u32[]{:S(2)}) collective-permute-start(bf16[80,768]{1,0:T(8,128)(2,1)S(1)} %collective-permute-done.7), channel_id=1, source_target_pairs={{0,32},{32,64},{64,96},{96,128},{128,160},{160,192},{192,224},{224... | collective-permute-start | bytes 368648 | tf_op jit(solution)/shard_map/ppermute | solution.py:119
  283.6 8.1 %collective-permute-start.9 = (bf16[80,768]{1,0:T(8,128)(2,1)S(1)}, bf16[80,768]{1,0:T(8,128)(2,1)S(1)}, u32[]{:S(2)}, u32[]{:S(2)}) collective-permute-start(bf16[80,768]{1,0:T(8,128)(2,1)S(1)} %collective-permute-done.8), channel_id=1, source_target_pairs={{0,32},{32,64},{64,96},{96,128},{128,160},{160,192},{192,224},{224... | collective-permute-start | bytes 368648 | tf_op jit(solution)/shard_map/ppermute | solution.py:119
  291.7 7.8 %collective-permute-start.10 = (bf16[80,768]{1,0:T(8,128)(2,1)S(1)}, bf16[80,768]{1,0:T(8,128)(2,1)S(1)}, u32[]{:S(2)}, u32[]{:S(2)}) collective-permute-start(bf16[80,768]{1,0:T(8,128)(2,1)S(1)} %collective-permute-done.9), channel_id=1, source_target_pairs={{0,32},{32,64},{64,96},{96,128},{128,160},{160,192},{192,224},{224... | collective-permute-start | bytes 368648 | tf_op jit(solution)/shard_map/ppermute | solution.py:119
  299.5 6.8 %collective-permute-start.11 = (bf16[80,768]{1,0:T(8,128)(2,1)S(1)}, bf16[80,768]{1,0:T(8,128)(2,1)S(1)}, u32[]{:S(2)}, u32[]{:S(2)}) collective-permute-start(bf16[80,768]{1,0:T(8,128)(2,1)S(1)} %collective-permute-done.10), channel_id=1, source_target_pairs={{0,32},{32,64},{64,96},{96,128},{128,160},{160,192},{192,224},{224... | collective-permute-start | bytes 368648 | tf_op jit(solution)/shard_map/ppermute | solution.py:119
  306.4 6.8 %collective-permute-start.12 = (bf16[80,768]{1,0:T(8,128)(2,1)S(1)}, bf16[80,768]{1,0:T(8,128)(2,1)S(1)}, u32[]{:S(2)}, u32[]{:S(2)}) collective-permute-start(bf16[80,768]{1,0:T(8,128)(2,1)S(1)} %collective-permute-done.11), channel_id=1, source_target_pairs={{0,32},{32,64},{64,96},{96,128},{128,160},{160,192},{192,224},{224... | collective-permute-start | bytes 368648 | tf_op jit(solution)/shard_map/ppermute | solution.py:119
  313.2 6.8 %collective-permute-start.13 = (bf16[80,768]{1,0:T(8,128)(2,1)S(1)}, bf16[80,768]{1,0:T(8,128)(2,1)S(1)}, u32[]{:S(2)}, u32[]{:S(2)}) collective-permute-start(bf16[80,768]{1,0:T(8,128)(2,1)S(1)} %collective-permute-done.12), channel_id=1, source_target_pairs={{0,32},{32,64},{64,96},{96,128},{128,160},{160,192},{192,224},{224... | collective-permute-start | bytes 368648 | tf_op jit(solution)/shard_map/ppermute | solution.py:119
  320.0 6.8 %collective-permute-start.14 = (bf16[80,768]{1,0:T(8,128)(2,1)S(1)}, bf16[80,768]{1,0:T(8,128)(2,1)S(1)}, u32[]{:S(2)}, u32[]{:S(2)}) collective-permute-start(bf16[80,768]{1,0:T(8,128)(2,1)S(1)} %collective-permute-done.13), channel_id=1, source_target_pairs={{0,32},{32,64},{64,96},{96,128},{128,160},{160,192},{192,224},{224... | collective-permute-start | bytes 368648 | tf_op jit(solution)/shard_map/ppermute | solution.py:119
  327.4 1.9 copy-start.3
  330.1 13.7 %collective-permute-start.16 = (bf16[256,768]{1,0:T(8,128)(2,1)S(1)}, bf16[256,768]{1,0:T(8,128)(2,1)S(1)}, u32[]{:S(2)}, u32[]{:S(2)}) collective-permute-start(bf16[256,768]{1,0:T(8,128)(2,1)S(1)} %get-tuple-element.10), channel_id=1, source_target_pairs={{0,16},{1,17},{2,18},{3,19},{4,20},{5,21},{6,22},{7,23},{8,24},{9,... | collective-permute-start | bytes 1179656 | tf_op jit(solution)/shard_map/ppermute | solution.py:10
  344.7 29.8 %copy-start.1 = (bf16[1280,768]{1,0:T(8,128)(2,1)S(1)}, bf16[1280,768]{1,0:T(8,128)(2,1)}, u32[]{:S(2)}) copy-start(bf16[1280,768]{1,0:T(8,128)(2,1)} %all-gather.5.cloned.1.call-done) | copy-start | bytes 5898244
  350.3 64.1 %all-to-all-start.4 = ((bf16[32,40,256]{2,1,0:T(8,128)(2,1)}), bf16[32,40,256]{2,1,0:T(8,128)(2,1)}, u32[]{:S(2)}, u32[]{:S(2)}) async-start(bf16[32,40,256]{2,1,0:T(8,128)(2,1)} %bitcast.78), calls=%async_computation.4 | async-start | bytes 1310720 | tf_op jit(solution)/shard_map/all_to_all | solution.py:130
  376.3 36.5 %copy-start.10 = (bf16[1,768,256]{2,1,0:T(8,128)(2,1)S(1)}, bf16[1,768,256]{2,1,0:T(8,128)(2,1)}, u32[]{:S(2)}) copy-start(bf16[1,768,256]{2,1,0:T(8,128)(2,1)} %param.14) | copy-start | bytes 1179652
  376.3 53.0 %copy-start.4 = (f32[256,768]{1,0:T(8,128)S(1)}, f32[256,768]{1,0:T(8,128)}, u32[]{:S(2)}) copy-start(f32[256,768]{1,0:T(8,128)} %get-tuple-element.9) | copy-start | bytes 2359300
  376.3 53.0 %collective-permute-start.15 = (bf16[256,768]{1,0:T(8,128)(2,1)}, bf16[256,768]{1,0:T(8,128)(2,1)}, u32[]{:S(2)}, u32[]{:S(2)}) collective-permute-start(bf16[256,768]{1,0:T(8,128)(2,1)} %get-tuple-element.8), channel_id=1, source_target_pairs={{0,16},{1,17},{2,18},{3,19},{4,20},{5,21},{6,22},{7,23},{8,24},{9,... | collective-permute-start | bytes 1179656 | tf_op jit(solution)/shard_map/ppermute | solution.py:10
  404.8 8.0 %copy-start.13 = (bf16[1280,768]{1,0:T(8,128)(2,1)S(1)}, bf16[1280,768]{1,0:T(8,128)(2,1)}, u32[]{:S(2)}) copy-start(bf16[1280,768]{1,0:T(8,128)(2,1)} %all-gather.3.cloned.1.call-done) | copy-start | bytes 5898244
  408.1 25.1 %copy-start.8 = (pred[1280,128]{1,0:T(8,128)(4,1)S(1)}, pred[1280,128]{1,0:T(8,128)(4,1)}, u32[]{:S(2)}) copy-start(pred[1280,128]{1,0:T(8,128)(4,1)} %copy-done.7) | copy-start | bytes 491524
  408.1 34.1 %copy-start.2 = (f32[1280,128]{1,0:T(8,128)S(1)}, f32[1280,128]{1,0:T(8,128)}, u32[]{:S(2)}) copy-start(f32[1280,128]{1,0:T(8,128)} %select_reduce_fusion) | copy-start | bytes 1966084
  408.1 23.2 %collective-permute-start.17 = (bf16[768,256]{1,0:T(8,128)(2,1)}, bf16[768,256]{1,0:T(8,128)(2,1)}, u32[]{:S(2)}, u32[]{:S(2)}) collective-permute-start(bf16[768,256]{1,0:T(8,128)(2,1)} %get-tuple-element.12), channel_id=1, source_target_pairs={{0,16},{1,17},{2,18},{3,19},{4,20},{5,21},{6,22},{7,23},{8,24},{9,... | collective-permute-start | bytes 1179656 | tf_op jit(solution)/shard_map/ppermute | solution.py:10
  414.4 27.8 %all-to-all-start.1 = ((bf16[32,40,256]{2,1,0:T(8,128)(2,1)}), bf16[32,40,256]{2,1,0:T(8,128)(2,1)S(1)}, u32[]{:S(2)}, u32[]{:S(2)}) async-start(bf16[32,40,256]{2,1,0:T(8,128)(2,1)} %bitcast.81), calls=%async_computation.1 | async-start | bytes 1310720 | tf_op jit(solution)/shard_map/all_to_all | solution.py:98
Sparse Core Ops, SparseCore 0:
  63.0 148.9 reduce-scatter.3
  214.9 68.4 all-gather.4
  322.1 82.6 all-gather.2
